TPU v7x, 32 devices: a whole 2x2x4 slice. The times are simulated.
32 devices in a mesh: groups: 2 (over y), people: 4 (over z), blocks: 2 (over x), sub: 2 (over core).
Axes of the slice: x: 2, y: 2, z: 4, core: 2. Of those that a mesh axis runs over, the one named last changes fastest.
Arguments:
- dosage: int32 [4096, 2048], P(('groups', 'people', 'sub'), 'blocks'), parts along dimension 0, may hold values from 0 to 200
- fold: int32 [4096], P(('groups', 'people', 'sub')), parts along dimension 0, may hold values from 0 to 1, as said below
- pheno: bfloat16 [4096, 48], P(('groups', 'people', 'sub')), parts along dimension 0, may hold values from -8 to 8
- ridges: float32 [5], replicated, may hold values from 1 to 20
Outputs:
- second: float32 [48, 5, 4096], P(('blocks', 'sub'), None, ('groups', 'people')), parts along dimension 2
There are 2 independent parts, one for each index of `groups`. A program takes and returns all parts, laid end to end along the dimension named above; an argument that names none is the same for every part. Nothing has to cross between parts.
Inputs may be any that keep to these rules, and one draw needn't show every extreme that they name: Each fold holds exactly 1024 people.
All inputs are finite; a program needn't handle non-finite values.
Results may differ from a plain program's by a relative error of at most 0.0021.
Values may be sent and summed in bfloat16 or wider, within the bound.
No kernel may reach another device: no remote copies, remote signals or barrier semaphores. Data moves between devices by JAX's collectives and lax.ppermute only.
A program may use at most 64 MiB of HBM per device.

v0:
```python
import jax
import jax.numpy as jnp
from jax import lax
from jax.sharding import PartitionSpec as P

TRAITS = 48
RIDGES = 5
FOLDS = 2
ITERS = 10
ITERS_TWO = 4
highest = lax.Precision.HIGHEST


def conjugate(apply_system, right_side, steps):
    estimate = jnp.zeros_like(right_side)
    residual = right_side
    direction = right_side
    current = jnp.sum(residual * residual, -2, keepdims=True)
    for step in range(steps):
        image = apply_system(direction)
        alpha = current / jnp.sum(direction * image, -2, keepdims=True)
        estimate = estimate + alpha * direction
        residual = residual - alpha * image
        following = jnp.sum(residual * residual, -2, keepdims=True)
        direction = residual + following / current * direction
        current = following
    return estimate


def covariance_rows(gram_rows, row_sums, all_sums, row_mean, all_mean, train_count):
    return (
        gram_rows
        - row_sums[:, None] * all_mean[None, :]
        - row_mean[:, None] * all_sums[None, :]
        + train_count * row_mean[:, None] * all_mean[None, :]
    )


def train_total(pieces, fold_index):
    return sum([pieces[other] for other in range(FOLDS) if other != fold_index])


def system_rows(shares, sums_all, column_mean, column_spread, row_start, share_rows, train_count):
    row_mean = lax.dynamic_slice_in_dim(column_mean, row_start, share_rows, 0)
    row_spread = lax.dynamic_slice_in_dim(column_spread, row_start, share_rows, 0)
    systems = []
    for fold_index in range(FOLDS):
        sums_train = train_total(sums_all, fold_index)
        row_sums = lax.dynamic_slice_in_dim(sums_train, row_start, share_rows, 0)
        covariance = covariance_rows(
            train_total(shares, fold_index),
            row_sums,
            sums_train,
            row_mean,
            column_mean,
            train_count,
        )
        systems.append(covariance / (train_count * row_spread[:, None] * column_spread[None, :]))
    return (jnp.stack(systems), row_spread)


def shards(dosage, fold, pheno, ridges):
    row_count, block_size = dosage.shape
    people_count = lax.axis_size("people")
    sub_count = lax.axis_size("sub")
    people = row_count * people_count * sub_count
    train_count = people - people // FOLDS
    centred = (dosage - 100).astype(jnp.bfloat16)
    pheno_wide = pheno.astype(jnp.float32)
    masks = [fold[:, None] == fold_index for fold_index in range(FOLDS)]
    grams, sums, squares, cross, totals = ([], [], [], [], [])
    for mask in masks:
        masked = jnp.where(mask, centred, jnp.zeros_like(centred))
        grams.append(
            lax.dot_general(
                masked, centred, (((0,), (0,)), ((), ())), preferred_element_type=jnp.float32
            )
        )
        masked_wide = masked.astype(jnp.float32)
        sums.append(jnp.sum(masked_wide, 0))
        squares.append(jnp.sum(masked_wide * masked_wide, 0))
        cross.append(
            lax.dot_general(
                masked, pheno, (((0,), (0,)), ((), ())), preferred_element_type=jnp.float32
            )
        )
        totals.append(jnp.sum(jnp.where(mask, pheno_wide, 0.0), 0))
    sums_all, squares_all, cross_all, totals_all = lax.psum(
        (jnp.stack(sums), jnp.stack(squares), jnp.stack(cross), jnp.stack(totals)),
        ("people", "sub"),
    )
    column_mean = sum([sums_all[fold_index] for fold_index in range(FOLDS)]) / people
    column_spread = jnp.sqrt(
        sum([squares_all[fold_index] for fold_index in range(FOLDS)]) / people
        - column_mean * column_mean
        + 1e-05
    )
    right_sides = []
    for fold_index in range(FOLDS):
        right_sides.append(
            (
                train_total(cross_all, fold_index)
                - column_mean[:, None] * train_total(totals_all, fold_index)[None, :]
            )
            / (train_count * column_spread[:, None])
        )
    gram_stack = jnp.stack(grams)
    share_rows = block_size // (people_count * sub_count)
    row_start = (lax.axis_index("people") * sub_count + lax.axis_index("sub")) * share_rows
    shares = lax.psum_scatter(gram_stack, ("people", "sub"), scatter_dimension=1, tiled=True)
    systems, row_spread = system_rows(
        shares, sums_all, column_mean, column_spread, row_start, share_rows, train_count
    )
    whole = lax.all_gather(systems, ("people", "sub"), axis=1, tiled=True)
    own_fold = lax.axis_index("sub")
    system = lax.dynamic_index_in_dim(whole, own_fold, 0, keepdims=False)
    trait_share = TRAITS // people_count
    trait_start = lax.axis_index("people") * trait_share
    right_own = lax.dynamic_index_in_dim(jnp.stack(right_sides), own_fold, 0, keepdims=False)
    right_cols = lax.dynamic_slice_in_dim(right_own, trait_start, trait_share, 1)
    shifts = jnp.repeat(ridges, trait_share)
    estimate = conjugate(
        lambda direction: jnp.dot(system, direction, precision=highest) + shifts * direction,
        jnp.tile(right_cols, (1, RIDGES)),
        ITERS,
    )
    scaled = (estimate / column_spread[:, None]).astype(jnp.bfloat16)
    scaled = scaled.reshape(block_size, RIDGES, trait_share)
    gathered = lax.all_gather(scaled[None], ("people", "sub"), axis=0, tiled=True)
    coefficients = gathered.reshape(people_count, sub_count, block_size, RIDGES, trait_share)
    coefficients = coefficients.transpose(1, 2, 3, 0, 4).reshape(FOLDS, block_size, RIDGES * TRAITS)
    prediction = jnp.zeros((row_count, RIDGES * TRAITS), jnp.float32)
    for fold_index in range(FOLDS):
        offset = jnp.dot(
            column_mean, coefficients[fold_index].astype(jnp.float32), precision=highest
        )
        outcome = (
            jnp.dot(centred, coefficients[fold_index], preferred_element_type=jnp.float32) - offset
        )
        prediction = prediction + jnp.where(masks[fold_index], outcome, 0.0)
    prediction = prediction.astype(jnp.bfloat16).reshape(1, row_count, RIDGES, TRAITS)
    moved, moved_pheno = (
        lax.all_to_all(prediction, ("blocks", "sub"), split_axis=3, concat_axis=0, tiled=True),
        lax.all_to_all(
            pheno[None, :, None, :], ("blocks", "sub"), split_axis=3, concat_axis=0, tiled=True
        ),
    )
    block_count = lax.axis_size("blocks")
    trait_group = TRAITS // (block_count * sub_count)
    predictors = moved.reshape(block_count, sub_count, row_count, RIDGES, trait_group)
    predictors = predictors.transpose(1, 2, 4, 0, 3).reshape(
        sub_count * row_count, trait_group, block_count * RIDGES
    )
    targets = moved_pheno.reshape(block_count, sub_count, row_count, trait_group)[0]
    targets = targets.reshape(sub_count * row_count, trait_group)
    gram_two = jnp.einsum(
        "nta,ntb->tab", predictors, predictors, preferred_element_type=jnp.float32
    )
    cross_two = jnp.einsum("nt,nta->ta", targets, predictors, preferred_element_type=jnp.float32)
    gram_two, cross_two = lax.psum((gram_two, cross_two), "people")
    gram_two = gram_two / people
    cross_two = cross_two / people
    predictor_count = block_count * RIDGES
    level = jnp.trace(gram_two, axis1=1, axis2=2) / predictor_count + 1e-06
    level_shift = ridges[None, None, :] * level[:, None, None]
    right_two = jnp.broadcast_to(cross_two[:, :, None], (trait_group, predictor_count, RIDGES))
    weights = conjugate(
        lambda direction: jnp.einsum("tab,tbr->tar", gram_two, direction, precision=highest)
        + level_shift * direction,
        right_two,
        ITERS_TWO,
    )
    return jnp.einsum("nta,tar->trn", predictors.astype(jnp.float32), weights, precision=highest)


def solution(mesh):
    return jax.shard_map(
        shards,
        mesh=mesh,
        in_specs=(
            P(("groups", "people", "sub"), "blocks"),
            P(("groups", "people", "sub")),
            P(("groups", "people", "sub"), None),
            P(),
        ),
        out_specs=P(("blocks", "sub"), None, ("groups", "people")),
        check_vma=False,
    )
```

profile of v0, /device:TPU:0, one launch (start us, length us, event | category | flops | bytes accessed | tf_op | source)
XLA Modules:
  0.0 376.7 jit_solution(10997729040896676900)
XLA Ops:
  6.5 0.7 broadcast_compare_fusion
  7.2 1.7 convert_reduce_fusion.1
  8.9 0.8 convolution_bitcast_fusion
  9.7 0.8 convolution_bitcast_fusion.1
  10.6 4.1 %pad_maximum_fusion = f32[2,1024,1024]{2,1,0:T(8,128)} fusion(f32[1,1024,1024]{2,1,0:T(8,128)S(1)} %convolution_bitcast_fusion, f32[1,1024,1024]{2,1,0:T(8,128)S(1)} %convolution_bitcast_fusion.1), kind=kLoop, calls=%fused_computation | loop fusion | flops 2097152 | bytes 16777216 | tf_op jit(solution)/shard_map/stack | solution.py:107
  14.7 0.6 copy-done
  15.9 0.8 pad_maximum_fusion.2
  17.0 31.8 %all-reduce = (f32[2,1024]{1,0:T(2,128)S(1)}, f32[2,1024]{1,0:T(2,128)S(1)}, f32[2,48]{1,0:T(2,128)S(1)}) all-reduce(f32[2,1024]{1,0:T(2,128)S(1)} %get-tuple-element.88, f32[2,1024]{1,0:T(2,128)S(1)} %get-tuple-element.87, f32[2,48]{1,0:T(2,128)S(1)} %pad_maximum_fusion.5), channel_id=1, replica_groups=mesh['groups'=2,'people'=4,'blocks'=2,'sub'=2] {'people','sub'}, use_global_device_ids=true, to_apply=%region_9.10 | all-reduce | flops 4192 | bytes 33536 | tf_op jit(solution)/shard_map/psum | solution.py:88
  49.0 58.6 %reduce-scatter.2.cloned.1.call-done = f32[2,128,1024]{2,1,0:T(8,128)} async-done(((f32[2,1024,1024]{2,1,0:T(8,128)}), f32[2,128,1024]{2,1,0:T(8,128)}) %reduce-scatter.2.cloned.1.call-update) | async-done | bytes 1048592 | tf_op jit(solution)/shard_map/reduce_scatter | solution.py:110
  107.6 1.7 multiply_divide_fusion.1
  109.3 1.2 pad_maximum_fusion.1
  110.5 0.5 broadcast.463
  111.0 0.8 reduce.4
  111.8 0.6 reshape.722
  112.4 3.8 %all-to-all-start.1 = ((bf16[4,2,1536]{2,1,0:T(2,128)(2,1)}), bf16[4,2,1536]{2,1,0:T(2,128)(2,1)S(1)}, u32[]{:S(2)}, u32[]{:S(2)}) async-start(bf16[4,2,1536]{2,1,0:T(2,128)(2,1)} %reshape.722), calls=%async_computation.2 | async-start | bytes 49152 | tf_op jit(solution)/shard_map/all_to_all | solution.py:144
  116.4 3.1 all-to-all-done.1
  119.6 44.7 %all-reduce.4.cloned.1.call-done = f32[2,1024,48]{1,2,0:T(8,128)} async-done(((f32[2,1024,48]{1,2,0:T(8,128)}), f32[2,1024,48]{1,2,0:T(8,128)}) %all-reduce.4.cloned.1.call-update) | async-done | bytes 393232 | tf_op jit(solution)/shard_map/psum | solution.py:88
  164.3 1.1 fusion.89
  165.9 81.2 %all-gather.2.cloned.1.call-done = f32[2,1024,1024]{2,1,0:T(8,128)} async-done(((f32[2,128,1024]{2,1,0:T(8,128)}), f32[2,1024,1024]{2,1,0:T(8,128)}) %all-gather.2.cloned.1.call-update) | async-done | bytes 8388624 | tf_op jit(solution)/shard_map/all_gather | solution.py:114
  247.1 6.4 %multiply_reduce_fusion.17 = (f32[60]{0:T(128)S(1)}, f32[1024,60]{0,1:T(8,128)S(1)}) fusion(f32[1024,60]{0,1:T(8,128)S(1)} %tile.16, f32[60]{0:T(128)S(1)} %mul.733, f32[2,1024,1024]{2,1,0:T(8,128)} %all-gather.2.cloned.1.call-done, s32[]{:T(128)S(6)} %select_n.49), kind=kOutput, calls=%fused_computation.123 | convolution fusion | flops 755220416 | bytes 4965108 | tf_op jit(solution)/shard_map/dot_general | solution.py:123
  253.9 6.5 %multiply_reduce_fusion.15 = (f32[60]{0:T(128)S(1)}, f32[1024,60]{0,1:T(8,128)S(1)}) fusion(f32[1024,60]{0,1:T(8,128)S(1)} %multiply_add_fusion.10, f32[60]{0:T(128)S(1)} %mul.733, f32[2,1024,1024]{2,1,0:T(8,128)} %all-gather.2.cloned.1.call-done, s32[]{:T(128)S(6)} %select_n.49), kind=kOutput, calls=%fused_computation.119 | convolution fusion | flops 755220416 | bytes 4965108 | tf_op jit(solution)/shard_map/dot_general | solution.py:123
  260.7 6.5 %multiply_reduce_fusion.13 = (f32[60]{0:T(128)S(1)}, f32[1024,60]{0,1:T(8,128)S(1)}) fusion(f32[1024,60]{0,1:T(8,128)S(1)} %multiply_add_fusion.9, f32[60]{0:T(128)S(1)} %mul.733, f32[2,1024,1024]{2,1,0:T(8,128)} %all-gather.2.cloned.1.call-done, s32[]{:T(128)S(6)} %select_n.49), kind=kOutput, calls=%fused_computation.115 | convolution fusion | flops 755220416 | bytes 4965108 | tf_op jit(solution)/shard_map/dot_general | solution.py:123
  267.5 6.6 %multiply_reduce_fusion.11 = (f32[60]{0:T(128)S(1)}, f32[1024,60]{0,1:T(8,128)S(1)}) fusion(f32[1024,60]{0,1:T(8,128)S(1)} %multiply_add_fusion.8, f32[60]{0:T(128)S(1)} %mul.733, f32[2,1024,1024]{2,1,0:T(8,128)} %all-gather.2.cloned.1.call-done, s32[]{:T(128)S(6)} %select_n.49), kind=kOutput, calls=%fused_computation.111 | convolution fusion | flops 755220416 | bytes 4965108 | tf_op jit(solution)/shard_map/dot_general | solution.py:123
  274.5 6.5 %multiply_reduce_fusion.9 = (f32[60]{0:T(128)S(1)}, f32[1024,60]{0,1:T(8,128)S(1)}) fusion(f32[1024,60]{0,1:T(8,128)S(1)} %multiply_add_fusion.7, f32[60]{0:T(128)S(1)} %mul.733, f32[2,1024,1024]{2,1,0:T(8,128)} %all-gather.2.cloned.1.call-done, s32[]{:T(128)S(6)} %select_n.49), kind=kOutput, calls=%fused_computation.107 | convolution fusion | flops 755220416 | bytes 4965108 | tf_op jit(solution)/shard_map/dot_general | solution.py:123
  281.3 6.5 %multiply_reduce_fusion.7 = (f32[60]{0:T(128)S(1)}, f32[1024,60]{0,1:T(8,128)S(1)}) fusion(f32[1024,60]{0,1:T(8,128)S(1)} %multiply_add_fusion.6, f32[60]{0:T(128)S(1)} %mul.733, f32[2,1024,1024]{2,1,0:T(8,128)} %all-gather.2.cloned.1.call-done, s32[]{:T(128)S(6)} %select_n.49), kind=kOutput, calls=%fused_computation.103 | convolution fusion | flops 755220416 | bytes 4965108 | tf_op jit(solution)/shard_map/dot_general | solution.py:123
  288.2 6.6 %multiply_reduce_fusion.5 = (f32[60]{0:T(128)S(1)}, f32[1024,60]{0,1:T(8,128)S(1)}) fusion(f32[1024,60]{0,1:T(8,128)S(1)} %multiply_add_fusion.5, f32[60]{0:T(128)S(1)} %mul.733, f32[2,1024,1024]{2,1,0:T(8,128)} %all-gather.2.cloned.1.call-done, s32[]{:T(128)S(6)} %select_n.49), kind=kOutput, calls=%fused_computation.99 | convolution fusion | flops 755220416 | bytes 4965108 | tf_op jit(solution)/shard_map/dot_general | solution.py:123
  295.1 6.8 %multiply_reduce_fusion.3 = (f32[60]{0:T(128)S(1)}, f32[1024,60]{0,1:T(8,128)S(1)}) fusion(f32[1024,60]{0,1:T(8,128)S(1)} %multiply_add_fusion.4, f32[60]{0:T(128)S(1)} %mul.733, f32[2,1024,1024]{2,1,0:T(8,128)} %all-gather.2.cloned.1.call-done, s32[]{:T(128)S(6)} %select_n.49), kind=kOutput, calls=%fused_computation.95 | convolution fusion | flops 755220416 | bytes 4965108 | tf_op jit(solution)/shard_map/dot_general | solution.py:123
  302.3 6.5 %multiply_reduce_fusion.1 = (f32[60]{0:T(128)S(1)}, f32[1024,60]{0,1:T(8,128)S(1)}) fusion(f32[1024,60]{0,1:T(8,128)S(1)} %multiply_add_fusion.3, f32[60]{0:T(128)S(1)} %mul.733, f32[2,1024,1024]{2,1,0:T(8,128)} %all-gather.2.cloned.1.call-done, s32[]{:T(128)S(6)} %select_n.49), kind=kOutput, calls=%fused_computation.91 | convolution fusion | flops 755220416 | bytes 4965108 | tf_op jit(solution)/shard_map/dot_general | solution.py:123
  309.0 4.3 %fusion.67 = f32[60]{0:T(128)S(1)} fusion(f32[2,1024,1024]{2,1,0:T(8,128)S(1)} %bitcast.162, s32[]{:T(128)S(6)} %select_n.49, f32[1024,60]{0,1:T(8,128)S(1)} %get-tuple-element.23, f32[1024,60]{0,1:T(8,128)S(1)} %multiply_add_fusion.3, f32[60]{0:T(128)S(1)} %div.291, f32[60]{0:T(128)S(1)} %mul.733), kind=kOutput, calls=%fused_computation.56 | convolution fusion | flops 755466176 | bytes 5244660 | tf_op jit(solution)/shard_map/dot_general | solution.py:123
  313.7 17.7 %all_gather.7 = bf16[8,1024,5,12]{1,3,2,0:T(8,128)(2,1)S(1)} all-gather(bf16[1,1024,5,12]{1,3,2,0:T(8,128)(2,1)S(1)} %broadcast_in_dim_reshape.2), channel_id=1, replica_groups=mesh['groups'=2,'people'=4,'blocks'=2,'sub'=2] {'people','sub'}, dimensions={0}, use_global_device_ids=true | all-gather | bytes 1105920 | tf_op jit(solution)/shard_map/all_gather | solution.py:129
  331.3 1.0 copy.84
  332.4 1.7 fusion.149
  334.1 0.5 copy.54
  334.8 0.5 fusion.124
  335.2 0.6 copy.55
  335.9 0.5 fusion.122
  336.4 0.4 fusion.65
  336.8 0.3 fusion.66
  337.1 0.7 copy.56
  337.8 3.4 all-to-all-start
  341.4 5.1 %all-to-all-done = bf16[1,256,5,48]{1,2,0,3:T(8,128)(2,1)S(1)} async-done(((bf16[1,256,5,48]{1,2,0,3:T(8,128)(2,1)}), bf16[1,256,5,48]{1,2,0,3:T(8,128)(2,1)S(1)}, u32[]{:S(2)}, u32[]{:S(2)}) %all-to-all-start) | async-done | bytes 122912 | tf_op jit(solution)/shard_map/all_to_all | solution.py:143
  347.1 18.9 %all-reduce.1 = (f32[12,10,10]{2,1,0:T(8,128)S(1)}, f32[12,10]{1,0:T(8,128)S(1)}) all-reduce(f32[12,10,10]{2,1,0:T(8,128)S(1)} %fusion.94, f32[12,10]{1,0:T(8,128)S(1)} %bitcast.176), channel_id=1, replica_groups=mesh['groups'=2,'people'=4,'blocks'=2,'sub'=2] {'people'}, use_global_device_ids=true, to_apply=%region_33.34 | all-reduce | flops 1320 | bytes 10560 | tf_op jit(solution)/shard_map/psum | solution.py:160
  366.4 0.4 multiply_reduce_fusion.23
  367.1 0.4 multiply_reduce_fusion.21
  367.8 0.4 multiply_reduce_fusion.19
  368.4 0.4 fusion.71
  368.8 0.3 fusion.90
  369.1 0.7 copy.65
  (101 shorter events, 7.0 us)
Async XLA Ops:
  6.5 101.0 %reduce-scatter.2.cloned.1.call-start = ((), (), s32[]{:S(2)}) async-start(), calls=%async_computation.4 | async-start | bytes 9437184 | tf_op jit(solution)/shard_map/reduce_scatter | solution.py:110
  14.6 0.7 copy-start
  14.7 101.6 %copy-start.1 = (f32[5]{0:T(128)S(1)}, f32[5]{0:T(128)}, u32[]{:S(2)}) copy-start(f32[5]{0:T(128)} %param.7) | copy-start | bytes 64
  14.7 149.7 %all-reduce.4.cloned.1.call-start = ((), (), s32[]{:S(2)}) async-start(), calls=%async_computation.3 | async-start | bytes 786432 | tf_op jit(solution)/shard_map/psum | solution.py:88
  16.7 230.3 %all-gather.2.cloned.1.call-start = ((), (), s32[]{:S(2)}) async-start(), calls=%async_computation.5 | async-start | bytes 9437184 | tf_op jit(solution)/shard_map/all_gather | solution.py:114
  112.4 7.1 %all-to-all-start.1 = ((bf16[4,2,1536]{2,1,0:T(2,128)(2,1)}), bf16[4,2,1536]{2,1,0:T(2,128)(2,1)S(1)}, u32[]{:S(2)}, u32[]{:S(2)}) async-start(bf16[4,2,1536]{2,1,0:T(2,128)(2,1)} %reshape.722), calls=%async_computation.2 | async-start | bytes 49152 | tf_op jit(solution)/shard_map/all_to_all | solution.py:144
  288.1 20.9 %slice-start = ((s8[8388608]{0:T(1024)(128)(4,1)}), s8[4194304]{0:T(1024)(128)(4,1)S(1)}, s32[]{:S(2)}) async-start(s8[8388608]{0:T(1024)(128)(4,1)} %bitcast.161), calls=%async_computation.6 | async-start | bytes 8388608
  295.1 13.9 %slice-start.1 = ((s8[8388608]{0:T(1024)(128)(4,1)}), s8[4194304]{0:T(1024)(128)(4,1)S(1)}, s32[]{:S(2)}) async-start(s8[8388608]{0:T(1024)(128)(4,1)} %bitcast.161), calls=%async_computation.7 | async-start | bytes 8388608
  337.8 8.6 %all-to-all-start = ((bf16[1,256,5,48]{1,2,0,3:T(8,128)(2,1)}), bf16[1,256,5,48]{1,2,0,3:T(8,128)(2,1)S(1)}, u32[]{:S(2)}, u32[]{:S(2)}) async-start(bf16[1,256,5,48]{1,2,0,3:T(8,128)(2,1)} %copy.56), calls=%async_computation.1 | async-start | bytes 393216 | tf_op jit(solution)/shard_map/all_to_all | solution.py:143
Sparse Core Ops, SparseCore 0:
  14.8 92.7 reduce-scatter.1
  109.9 54.3 all-reduce.3
  166.0 81.0 all-gather.1
where the time goes:
time: 381 us; the launch traced here: 377 us
  waiting for transfers between devices  193 us (51%)
  matrix products  69.3 us (18%)
  blocking collectives  68.3 us (18%)
  other arithmetic  16.9 us (4%)
  between operations  14 us (4%)
  local copies, waits for them, and re-layouts  8.12 us (2%)
  starting transfers between devices  7.23 us (2%)
    all_gather x1, waiting for transfers between devices, shards(): whole = lax.all_gather(systems, ('people', 'sub'), axis=1, tiled=True)  81.2 us
    dot_general x10, matrix products, shards(): jnp.dot(system, direction, precision=highest) + shifts * direction  63.1 us
    reduce_scatter x1, waiting for transfers between devices, shards(): lax.psum_scatter(gram_stack, ('people', 'sub'), scatter_dimension=1, tile...  58.6 us
    psum x1, waiting for transfers between devices, shards(): lax.psum((jnp.stack(sums), jnp.stack(squares), jnp.stack(cross), jnp.stac...  44.7 us
    psum x1, blocking collectives, shards(): lax.psum((jnp.stack(sums), jnp.stack(squares), jnp.stack(cross), jnp.stac...  31.8 us
    psum x1, blocking collectives, shards(): gram_two, cross_two = lax.psum((gram_two, cross_two), 'people')  18.9 us
    all_gather x1, blocking collectives, shards(): lax.all_gather(scaled[None], ('people', 'sub'), axis=0, tiled=True)  17.7 us
  transfers between devices with their start and end apart: 5, of which 5 were waited for; matrix products, arithmetic and copies ran while one was open for 2% of the time, Pallas kernels for 0%

commit v1 on v0

--- a/solution.py
+++ b/solution.py
@@ -9,6 +9,28 @@
 ITERS = 10
 ITERS_TWO = 4
 highest = lax.Precision.HIGHEST
+
+
+def in_order(blocks, dim):
+    dims = list(blocks.shape[1:])
+    dims[dim] *= blocks.shape[0]
+    return jnp.moveaxis(blocks, 0, dim).reshape(dims)
+
+
+def collect(x, axis, dim):
+    count = lax.axis_size(axis)
+    pairs = [(i, (i + 1) % count) for i in range(count)]
+    back = [(b, a) for a, b in pairs]
+    lower, upper = ([], [])
+    for step in range(count - 1):
+        if step % 2 == 0:
+            lower.append(lax.ppermute(lower[-1] if lower else x, axis, pairs))
+        else:
+            upper.append(lax.ppermute(upper[-1] if upper else x, axis, back))
+    blocks = jnp.stack([*lower[::-1], x, *upper])
+    shift = lax.axis_index(axis) - len(lower)
+    blocks = blocks[(jnp.arange(count) - shift) % count]
+    return in_order(blocks, dim)
 
 
 def conjugate(apply_system, right_side, steps):
@@ -111,7 +133,7 @@
     systems, row_spread = system_rows(
         shares, sums_all, column_mean, column_spread, row_start, share_rows, train_count
     )
-    whole = lax.all_gather(systems, ("people", "sub"), axis=1, tiled=True)
+    whole = collect(systems, ("people", "sub"), 1)
     own_fold = lax.axis_index("sub")
     system = lax.dynamic_index_in_dim(whole, own_fold, 0, keepdims=False)
     trait_share = TRAITS // people_count

time: 381 us -> 395 us (1.037)
  local copies, waits for them, and re-layouts: 8.12 us -> 34.6 us
  waiting for transfers between devices: 193 us -> 176 us
  starting transfers between devices: 7.23 us -> 14.1 us
  matrix products: 69.3 us -> 65.2 us
    all_gather x1 -> x0, waiting for transfers between devices: 81.2 us -> none  [shards(): whole = lax.all_gather(systems, ('people', 'sub'), axis=1, tiled=True)]
    ppermute x0 -> x7, waiting for transfers between devices: none -> 57.7 us  [the longest x4 57.7 us: collect(): lower.append(lax.ppermute(lower[-1] if lower else x, axis, pairs))]
    unnamed x11 -> x21, local copies, waits for them, and re-layouts: 1.83 us -> 15.6 us
    gather x0 -> x1, local copies, waits for them, and re-layouts: none -> 7.67 us  [collect(): blocks = blocks[(jnp.arange(count) - shift) % count]]
    ppermute x0 -> x7, starting transfers between devices: none -> 7.44 us  [the longest x3 7.37 us: collect(): upper.append(lax.ppermute(upper[-1] if upper else x, axis, back))]
    psum x1, waiting for transfers between devices: 44.7 us -> 49.8 us  [shards(): lax.psum((jnp.stack(sums), jnp.stack(squares), jnp.stack(cross), jnp.stac...]
    transpose x0 -> x1, local copies, waits for them, and re-layouts: none -> 4.23 us  [in_order(): return jnp.moveaxis(blocks, 0, dim).reshape(dims)]
    dot_general x10, matrix products: 63.1 us -> 59 us  [shards(): jnp.dot(system, direction, precision=highest) + shifts * direction]
  transfers between devices with their start and end apart: 5 -> 11, of which waited for: 5 -> 7; matrix products, arithmetic and copies ran while one was open for 2% -> 5% of each run, Pallas kernels for 0% -> 0%
where the time goes in v1:
time: 395 us; the launch traced here: 390 us
  waiting for transfers between devices  176 us (45%)
  blocking collectives  68.2 us (17%)
  matrix products  65.2 us (17%)
  local copies, waits for them, and re-layouts  34.6 us (9%)
  other arithmetic  16.9 us (4%)
  between operations  14.3 us (4%)
  starting transfers between devices  14.1 us (4%)
    reduce_scatter x1, waiting for transfers between devices, shards(): lax.psum_scatter(gram_stack, ('people', 'sub'), scatter_dimension=1, tile...  60.1 us
    dot_general x10, matrix products, shards(): jnp.dot(system, direction, precision=highest) + shifts * direction  59 us
    ppermute x4, waiting for transfers between devices, collect(): lower.append(lax.ppermute(lower[-1] if lower else x, axis, pairs))  57.7 us
    psum x1, waiting for transfers between devices, shards(): lax.psum((jnp.stack(sums), jnp.stack(squares), jnp.stack(cross), jnp.stac...  49.8 us
    psum x1, blocking collectives, shards(): lax.psum((jnp.stack(sums), jnp.stack(squares), jnp.stack(cross), jnp.stac...  31.7 us
    psum x1, blocking collectives, shards(): gram_two, cross_two = lax.psum((gram_two, cross_two), 'people')  19.2 us
    all_gather x1, blocking collectives, shards(): lax.all_gather(scaled[None], ('people', 'sub'), axis=0, tiled=True)  17.4 us
    unnamed x21, local copies, waits for them, and re-layouts  15.6 us
  transfers between devices with their start and end apart: 11, of which 7 were waited for; matrix products, arithmetic and copies ran while one was open for 5% of the time, Pallas kernels for 0%

profile of v1, /device:TPU:0, one launch (start us, length us, event | category | flops | bytes accessed | tf_op | source)
XLA Modules:
  0.0 389.6 jit_solution(16224117206466757311)
XLA Ops:
  6.5 0.7 broadcast_compare_fusion
  7.2 1.7 convert_reduce_fusion.1
  8.9 0.8 convolution_bitcast_fusion
  9.7 0.8 convolution_bitcast_fusion.1
  10.6 4.1 %pad_maximum_fusion = f32[2,1024,1024]{2,1,0:T(8,128)} fusion(f32[1,1024,1024]{2,1,0:T(8,128)S(1)} %convolution_bitcast_fusion, f32[1,1024,1024]{2,1,0:T(8,128)S(1)} %convolution_bitcast_fusion.1), kind=kLoop, calls=%fused_computation.1 | loop fusion | flops 2097152 | bytes 16777216 | tf_op jit(solution)/shard_map/stack | solution.py:129
  15.5 31.7 %all-reduce = (f32[2,1024]{1,0:T(2,128)S(1)}, f32[2,1024]{1,0:T(2,128)S(1)}, f32[2,48]{1,0:T(2,128)S(1)}) all-reduce(f32[2,1024]{1,0:T(2,128)S(1)} %get-tuple-element.88, f32[2,1024]{1,0:T(2,128)S(1)} %get-tuple-element.87, f32[2,48]{1,0:T(2,128)S(1)} %pad_maximum_fusion.5), channel_id=1, replica_groups=mesh['groups'=2,'people'=4,'blocks'=2,'sub'=2] {'people','sub'}, use_global_device_ids=true, to_apply=%region_9.10 | all-reduce | flops 4192 | bytes 33536 | tf_op jit(solution)/shard_map/psum | solution.py:110
  47.4 60.1 %reduce-scatter.2.cloned.1.call-done = f32[2,128,1024]{2,1,0:T(8,128)} async-done(((f32[2,1024,1024]{2,1,0:T(8,128)}), f32[2,128,1024]{2,1,0:T(8,128)}) %reduce-scatter.2.cloned.1.call-update) | async-done | bytes 1048592 | tf_op jit(solution)/shard_map/reduce_scatter | solution.py:132
  107.6 1.7 multiply_divide_fusion.1
  109.4 16.0 %collective-permute-done = f32[2,128,1024]{2,1,0:T(8,128)S(1)} collective-permute-done((f32[2,128,1024]{2,1,0:T(8,128)S(1)}, f32[2,128,1024]{2,1,0:T(8,128)S(1)}, u32[]{:S(2)}, u32[]{:S(2)}) %collective-permute-start) | collective-permute-done | bytes 1048608 | tf_op jit(solution)/shard_map/ppermute | solution.py:27
  125.4 3.5 collective-permute-start.4
  129.0 21.4 %collective-permute-done.1 = f32[2,128,1024]{2,1,0:T(8,128)S(1)} collective-permute-done((f32[2,128,1024]{2,1,0:T(8,128)S(1)}, f32[2,128,1024]{2,1,0:T(8,128)S(1)}, u32[]{:S(2)}, u32[]{:S(2)}) %collective-permute-start.1) | collective-permute-done | bytes 1048608 | tf_op jit(solution)/shard_map/ppermute | solution.py:27
  150.3 1.0 copy-done.1
  151.9 3.6 collective-permute-start.5
  155.5 20.3 %collective-permute-done.2 = f32[2,128,1024]{2,1,0:T(8,128)} collective-permute-done((f32[2,128,1024]{2,1,0:T(8,128)S(1)}, f32[2,128,1024]{2,1,0:T(8,128)}, u32[]{:S(2)}, u32[]{:S(2)}) %collective-permute-start.2) | collective-permute-done | bytes 1048608 | tf_op jit(solution)/shard_map/ppermute | solution.py:27
  175.8 0.8 pad_maximum_fusion.2
  177.2 0.8 reduce.4
  178.6 3.3 all-to-all-start.1
  182.1 3.6 all-to-all-done.1
  185.7 49.8 %all-reduce.4.cloned.1.call-done = f32[2,1024,48]{1,2,0:T(8,128)} async-done(((f32[2,1024,48]{1,2,0:T(8,128)}), f32[2,1024,48]{1,2,0:T(8,128)}) %all-reduce.4.cloned.1.call-update) | async-done | bytes 393232 | tf_op jit(solution)/shard_map/psum | solution.py:110
  235.5 1.1 fusion.89
  237.3 2.3 bitcast_dynamic-update-slice_fusion.7
  239.6 2.4 bitcast_dynamic-update-slice_fusion.6
  242.0 2.3 bitcast_dynamic-update-slice_fusion.5
  244.3 1.1 bitcast_dynamic-update-slice_fusion.4
  245.3 1.0 bitcast_dynamic-update-slice_fusion.3
  246.4 2.4 bitcast_dynamic-update-slice_fusion.2
  248.7 2.3 bitcast_dynamic-update-slice_fusion.1
  251.1 1.1 bitcast_dynamic-update-slice_fusion
  252.2 7.7 %gather_fusion = f32[8,2,128,1024]{3,2,1,0:T(8,128)} fusion(f32[8,2,128,1024]{3,2,1,0:T(8,128)} %bitcast_dynamic-update-slice_fusion, s32[1024]{0:T(1024)S(1)} %pad_clamp_fusion), kind=kCustom, calls=%fused_computation | custom fusion | bytes 16777248 | tf_op jit(solution)/shard_map/gather | solution.py:32
  259.8 4.2 %copy.57 = f32[2,8,128,1024]{3,2,1,0:T(8,128)S(1)} copy(f32[2,8,128,1024]{3,2,0,1:T(8,128)} %bitcast.193) | data formatting | bytes 16777216 | tf_op jit(solution)/shard_map/transpose | solution.py:17
  264.1 4.3 %multiply_reduce_fusion.17 = (f32[60]{0:T(128)S(1)}, f32[1024,60]{0,1:T(8,128)S(1)}) fusion(f32[1024,60]{0,1:T(8,128)S(1)} %tile.16, f32[60]{0:T(128)S(1)} %mul.734, f32[2,1024,1024]{2,1,0:T(8,128)S(1)} %bitcast.181, s32[]{:T(128)S(6)} %select_n.73), kind=kOutput, calls=%fused_computation.132 | convolution fusion | flops 755220416 | bytes 4965108 | tf_op jit(solution)/shard_map/dot_general | solution.py:145
  268.7 4.3 %multiply_reduce_fusion.15 = (f32[60]{0:T(128)S(1)}, f32[1024,60]{0,1:T(8,128)S(1)}) fusion(f32[1024,60]{0,1:T(8,128)S(1)} %multiply_add_fusion.10, f32[60]{0:T(128)S(1)} %mul.734, f32[2,1024,1024]{2,1,0:T(8,128)S(1)} %bitcast.182, s32[]{:T(128)S(6)} %select_n.73), kind=kOutput, calls=%fused_computation.128 | convolution fusion | flops 755220416 | bytes 4965108 | tf_op jit(solution)/shard_map/dot_general | solution.py:145
  273.4 6.5 %multiply_reduce_fusion.13 = (f32[60]{0:T(128)S(1)}, f32[1024,60]{0,1:T(8,128)S(1)}) fusion(f32[1024,60]{0,1:T(8,128)S(1)} %multiply_add_fusion.9, f32[60]{0:T(128)S(1)} %mul.734, f32[2,1024,1024]{2,1,0:T(8,128)} %bitcast.183, s32[]{:T(128)S(6)} %select_n.73), kind=kOutput, calls=%fused_computation.124 | convolution fusion | flops 755220416 | bytes 4965108 | tf_op jit(solution)/shard_map/dot_general | solution.py:145
  280.2 6.7 %multiply_reduce_fusion.11 = (f32[60]{0:T(128)S(1)}, f32[1024,60]{0,1:T(8,128)S(1)}) fusion(f32[1024,60]{0,1:T(8,128)S(1)} %multiply_add_fusion.8, f32[60]{0:T(128)S(1)} %mul.734, f32[2,1024,1024]{2,1,0:T(8,128)} %bitcast.184, s32[]{:T(128)S(6)} %select_n.73), kind=kOutput, calls=%fused_computation.120 | convolution fusion | flops 755220416 | bytes 4965108 | tf_op jit(solution)/shard_map/dot_general | solution.py:145
  287.2 6.5 %multiply_reduce_fusion.9 = (f32[60]{0:T(128)S(1)}, f32[1024,60]{0,1:T(8,128)S(1)}) fusion(f32[1024,60]{0,1:T(8,128)S(1)} %multiply_add_fusion.7, f32[60]{0:T(128)S(1)} %mul.734, f32[2,1024,1024]{2,1,0:T(8,128)} %bitcast.185, s32[]{:T(128)S(6)} %select_n.73), kind=kOutput, calls=%fused_computation.116 | convolution fusion | flops 755220416 | bytes 4965108 | tf_op jit(solution)/shard_map/dot_general | solution.py:145
  294.1 6.5 %multiply_reduce_fusion.7 = (f32[60]{0:T(128)S(1)}, f32[1024,60]{0,1:T(8,128)S(1)}) fusion(f32[1024,60]{0,1:T(8,128)S(1)} %multiply_add_fusion.6, f32[60]{0:T(128)S(1)} %mul.734, f32[2,1024,1024]{2,1,0:T(8,128)} %bitcast.186, s32[]{:T(128)S(6)} %select_n.73), kind=kOutput, calls=%fused_computation.112 | convolution fusion | flops 755220416 | bytes 4965108 | tf_op jit(solution)/shard_map/dot_general | solution.py:145
  300.9 7.0 %multiply_reduce_fusion.5 = (f32[60]{0:T(128)S(1)}, f32[1024,60]{0,1:T(8,128)S(1)}) fusion(f32[1024,60]{0,1:T(8,128)S(1)} %multiply_add_fusion.5, f32[60]{0:T(128)S(1)} %mul.734, f32[2,1024,1024]{2,1,0:T(8,128)} %bitcast.187, s32[]{:T(128)S(6)} %select_n.73), kind=kOutput, calls=%fused_computation.108 | convolution fusion | flops 755220416 | bytes 4965108 | tf_op jit(solution)/shard_map/dot_general | solution.py:145
  308.3 6.6 %multiply_reduce_fusion.3 = (f32[60]{0:T(128)S(1)}, f32[1024,60]{0,1:T(8,128)S(1)}) fusion(f32[1024,60]{0,1:T(8,128)S(1)} %multiply_add_fusion.4, f32[60]{0:T(128)S(1)} %mul.734, f32[2,1024,1024]{2,1,0:T(8,128)} %bitcast.188, s32[]{:T(128)S(6)} %select_n.73), kind=kOutput, calls=%fused_computation.104 | convolution fusion | flops 755220416 | bytes 4965108 | tf_op jit(solution)/shard_map/dot_general | solution.py:145
  315.2 6.5 %multiply_reduce_fusion.1 = (f32[60]{0:T(128)S(1)}, f32[1024,60]{0,1:T(8,128)S(1)}) fusion(f32[1024,60]{0,1:T(8,128)S(1)} %multiply_add_fusion.3, f32[60]{0:T(128)S(1)} %mul.734, f32[2,1024,1024]{2,1,0:T(8,128)} %bitcast.189, s32[]{:T(128)S(6)} %select_n.73), kind=kOutput, calls=%fused_computation.100 | convolution fusion | flops 755220416 | bytes 4965108 | tf_op jit(solution)/shard_map/dot_general | solution.py:145
  322.0 4.3 %fusion.67 = f32[60]{0:T(128)S(1)} fusion(f32[2,1024,1024]{2,1,0:T(8,128)S(1)} %bitcast.192, s32[]{:T(128)S(6)} %select_n.73, f32[1024,60]{0,1:T(8,128)S(1)} %get-tuple-element.23, f32[1024,60]{0,1:T(8,128)S(1)} %multiply_add_fusion.3, f32[60]{0:T(128)S(1)} %div.291, f32[60]{0:T(128)S(1)} %mul.734), kind=kOutput, calls=%fused_computation.57 | convolution fusion | flops 755466176 | bytes 5244660 | tf_op jit(solution)/shard_map/dot_general | solution.py:145
  326.6 17.4 %all_gather.3 = bf16[8,1024,5,12]{1,3,2,0:T(8,128)(2,1)S(1)} all-gather(bf16[1,1024,5,12]{1,3,2,0:T(8,128)(2,1)S(1)} %broadcast_in_dim_reshape.2), channel_id=1, replica_groups=mesh['groups'=2,'people'=4,'blocks'=2,'sub'=2] {'people','sub'}, dimensions={0}, use_global_device_ids=true | all-gather | bytes 1105920 | tf_op jit(solution)/shard_map/all_gather | solution.py:151
  344.0 1.0 copy.89
  345.0 1.5 fusion.151
  349.5 0.7 copy.61
  350.2 3.4 all-to-all-start
  353.8 5.1 %all-to-all-done = bf16[1,256,5,48]{1,2,0,3:T(8,128)(2,1)S(1)} async-done(((bf16[1,256,5,48]{1,2,0,3:T(8,128)(2,1)}), bf16[1,256,5,48]{1,2,0,3:T(8,128)(2,1)S(1)}, u32[]{:S(2)}, u32[]{:S(2)}) %all-to-all-start) | async-done | bytes 122912 | tf_op jit(solution)/shard_map/all_to_all | solution.py:165
  359.5 19.2 %all-reduce.1 = (f32[12,10,10]{2,1,0:T(8,128)S(1)}, f32[12,10]{1,0:T(8,128)S(1)}) all-reduce(f32[12,10,10]{2,1,0:T(8,128)S(1)} %fusion.94, f32[12,10]{1,0:T(8,128)S(1)} %bitcast.207), channel_id=1, replica_groups=mesh['groups'=2,'people'=4,'blocks'=2,'sub'=2] {'people'}, use_global_device_ids=true, to_apply=%region_33.34 | all-reduce | flops 1320 | bytes 10560 | tf_op jit(solution)/shard_map/psum | solution.py:182
  381.8 0.7 copy.70
  (128 shorter events, 13.9 us)
Async XLA Ops:
  6.5 101.1 %reduce-scatter.2.cloned.1.call-start = ((), (), s32[]{:S(2)}) async-start(), calls=%async_computation.4 | async-start | bytes 9437184 | tf_op jit(solution)/shard_map/reduce_scatter | solution.py:132
  14.6 0.7 copy-start.2
  14.6 167.3 %copy-start.3 = (f32[5]{0:T(128)S(1)}, f32[5]{0:T(128)}, u32[]{:S(2)}) copy-start(f32[5]{0:T(128)} %param.7) | copy-start | bytes 64
  14.7 220.8 %all-reduce.4.cloned.1.call-start = ((), (), s32[]{:S(2)}) async-start(), calls=%async_computation.3 | async-start | bytes 786432 | tf_op jit(solution)/shard_map/psum | solution.py:110
  109.4 16.1 %collective-permute-start = (f32[2,128,1024]{2,1,0:T(8,128)S(1)}, f32[2,128,1024]{2,1,0:T(8,128)S(1)}, u32[]{:S(2)}, u32[]{:S(2)}) collective-permute-start(f32[2,128,1024]{2,1,0:T(8,128)S(1)} %pad_maximum_fusion.1), channel_id=1, source_target_pairs={{0,1},{1,4},{4,5},{5,8},{8,9},{9,12},{12,13},{13,0},{2,3},{3,6},{6... | collective-permute-start | bytes 3145736 | tf_op jit(solution)/shard_map/ppermute | solution.py:27
  125.4 24.9 %collective-permute-start.1 = (f32[2,128,1024]{2,1,0:T(8,128)S(1)}, f32[2,128,1024]{2,1,0:T(8,128)S(1)}, u32[]{:S(2)}, u32[]{:S(2)}) collective-permute-start(f32[2,128,1024]{2,1,0:T(8,128)S(1)} %collective-permute-done), channel_id=1, source_target_pairs={{0,1},{1,4},{4,5},{5,8},{8,9},{9,12},{12,13},{13,0},{2,3},{3,6},{6... | collective-permute-start | bytes 3145736 | tf_op jit(solution)/shard_map/ppermute | solution.py:27
  125.4 26.4 %collective-permute-start.4 = (f32[2,128,1024]{2,1,0:T(8,128)S(1)}, f32[2,128,1024]{2,1,0:T(8,128)}, u32[]{:S(2)}, u32[]{:S(2)}) collective-permute-start(f32[2,128,1024]{2,1,0:T(8,128)S(1)} %pad_maximum_fusion.1), channel_id=1, source_target_pairs={{1,0},{4,1},{5,4},{8,5},{9,8},{12,9},{13,12},{0,13},{3,2},{6,3},{7... | collective-permute-start | bytes 3145736 | tf_op jit(solution)/shard_map/ppermute | solution.py:29
  150.3 1.0 copy-start.1
  151.3 24.5 %collective-permute-start.2 = (f32[2,128,1024]{2,1,0:T(8,128)S(1)}, f32[2,128,1024]{2,1,0:T(8,128)}, u32[]{:S(2)}, u32[]{:S(2)}) collective-permute-start(f32[2,128,1024]{2,1,0:T(8,128)S(1)} %collective-permute-done.1), channel_id=1, source_target_pairs={{0,1},{1,4},{4,5},{5,8},{8,9},{9,12},{12,13},{13,0},{2,3},{3,6},{6... | collective-permute-start | bytes 3145736 | tf_op jit(solution)/shard_map/ppermute | solution.py:27
  151.9 85.1 %collective-permute-start.5 = (f32[2,128,1024]{2,1,0:T(8,128)}, f32[2,128,1024]{2,1,0:T(8,128)}, u32[]{:S(2)}, u32[]{:S(2)}) collective-permute-start(f32[2,128,1024]{2,1,0:T(8,128)} %collective-permute-done.4), channel_id=1, source_target_pairs={{1,0},{4,1},{5,4},{8,5},{9,8},{12,9},{13,12},{0,13},{3,2},{6,3},{7... | collective-permute-start | bytes 3145736 | tf_op jit(solution)/shard_map/ppermute | solution.py:29
  175.8 61.4 %collective-permute-start.3 = (f32[2,128,1024]{2,1,0:T(8,128)}, f32[2,128,1024]{2,1,0:T(8,128)}, u32[]{:S(2)}, u32[]{:S(2)}) collective-permute-start(f32[2,128,1024]{2,1,0:T(8,128)} %collective-permute-done.2), channel_id=1, source_target_pairs={{0,1},{1,4},{4,5},{5,8},{8,9},{9,12},{12,13},{13,0},{2,3},{3,6},{6... | collective-permute-start | bytes 3145736 | tf_op jit(solution)/shard_map/ppermute | solution.py:27
  178.6 7.1 %all-to-all-start.1 = ((bf16[4,2,1536]{2,1,0:T(2,128)(2,1)}), bf16[4,2,1536]{2,1,0:T(2,128)(2,1)S(1)}, u32[]{:S(2)}, u32[]{:S(2)}) async-start(bf16[4,2,1536]{2,1,0:T(2,128)(2,1)} %reshape.783), calls=%async_computation.2 | async-start | bytes 49152 | tf_op jit(solution)/shard_map/all_to_all | solution.py:166
  237.0 14.1 %collective-permute-start.6 = (f32[2,128,1024]{2,1,0:T(8,128)}, f32[2,128,1024]{2,1,0:T(8,128)S(1)}, u32[]{:S(2)}, u32[]{:S(2)}) collective-permute-start(f32[2,128,1024]{2,1,0:T(8,128)} %collective-permute-done.5), channel_id=1, source_target_pairs={{1,0},{4,1},{5,4},{8,5},{9,8},{12,9},{13,12},{0,13},{3,2},{6,3},{7... | collective-permute-start | bytes 3145736 | tf_op jit(solution)/shard_map/ppermute | solution.py:29
  264.1 9.3 %copy-start = (f32[2,8,128,1024]{3,2,1,0:T(8,128)}, f32[2,8,128,1024]{3,2,1,0:T(8,128)S(1)}, u32[]{:S(2)}) copy-start(f32[2,8,128,1024]{3,2,1,0:T(8,128)S(1)} %copy.57) | copy-start | bytes 25165828
  300.9 21.1 %slice-start = ((s8[8388608]{0:T(1024)(128)(4,1)}), s8[4194304]{0:T(1024)(128)(4,1)S(1)}, s32[]{:S(2)}) async-start(s8[8388608]{0:T(1024)(128)(4,1)} %bitcast.190), calls=%async_computation.5 | async-start | bytes 8388608
  308.2 13.7 %slice-start.1 = ((s8[8388608]{0:T(1024)(128)(4,1)}), s8[4194304]{0:T(1024)(128)(4,1)S(1)}, s32[]{:S(2)}) async-start(s8[8388608]{0:T(1024)(128)(4,1)} %bitcast.190), calls=%async_computation.6 | async-start | bytes 8388608
  350.2 8.6 %all-to-all-start = ((bf16[1,256,5,48]{1,2,0,3:T(8,128)(2,1)}), bf16[1,256,5,48]{1,2,0,3:T(8,128)(2,1)S(1)}, u32[]{:S(2)}, u32[]{:S(2)}) async-start(bf16[1,256,5,48]{1,2,0,3:T(8,128)(2,1)} %copy.61), calls=%async_computation.1 | async-start | bytes 393216 | tf_op jit(solution)/shard_map/all_to_all | solution.py:165
Sparse Core Ops, SparseCore 0:
  14.8 92.7 reduce-scatter.1
  176.7 58.7 all-reduce.3
